TPU v7x, 32 devices: a whole 2x2x4 slice. The times are simulated.
32 devices in a mesh: replica: 8 (over z, y), tp: 4 (over x, core).
Axes of the slice: x: 2, y: 2, z: 4, core: 2. Of those that a mesh axis runs over, the one named last changes fastest.
Arguments:
- hidden: bfloat16 [96, 4, 8192], P('replica', None, 'tp'), may hold values from -6 to 6
- norm_gain: float32 [8192], replicated, may hold values from 0.5 to 1.5
- w_query: float32 [8192, 4096], P(('replica', 'tp')), may hold values from -0.0625 to 0.0625
- w_key: float32 [8192, 512], P(('replica', 'tp')), may hold values from -0.0625 to 0.0625
- w_value: float32 [8192, 512], P(('replica', 'tp')), may hold values from -0.0625 to 0.0625
- bias_query: float32 [4096], P('tp'), may hold values from -3 to 3
- bias_key: float32 [512], P('tp'), may hold values from -3 to 3
- bias_value: float32 [512], P('tp'), may hold values from -3 to 3
- key_pages: bfloat16 [512, 4, 128, 128], P(('replica', 'tp')), may hold values from -256 to 256
- value_pages: bfloat16 [512, 4, 128, 128], P(('replica', 'tp')), may hold values from -6 to 6
- kv_lengths: int32 [96], P(('replica', 'tp')), may hold values from 1 to 1024, as said below
- page_table: int32 [96, 8], P(('replica', 'tp')), may hold values from 0 to 15, as said below
Outputs:
- attended: bfloat16 [96, 4, 4096], P(('replica', 'tp'))
Inputs may be any that keep to these rules, and one draw needn't show every extreme that they name: `kv_lengths`: on every device, one row has exactly 1024 cached tokens. `page_table`: page ids are local to the pool of 16 pages of the device that holds the row. The first ceil(kv_lengths / 128) entries of a row name its pages in order; no page serves two of those entries on one device; later entries are arbitrary pages of the pool.
All inputs are finite; a program needn't handle non-finite values.
Results may differ from a plain program's by a relative error of at most 0.04.
Values may be sent and summed in bfloat16 or wider, within the bound.
No kernel may reach another device: no remote copies, remote signals or barrier semaphores. Data moves between devices by JAX's collectives and lax.ppermute only.
A program may use at most 128 MiB of HBM per device.

v0:
```python
import jax
import jax.numpy as jnp
from jax import lax
from jax.sharding import PartitionSpec as P

HD = 128
HQ = 32
KVH = 4
PAGE = 128
MOSTP = 8
EPS = 1e-06
THETA = 1000000.0


def rotate(values, positions):
    half = values.shape[-1] // 2
    freq = THETA ** (-(jnp.arange(half, dtype=jnp.float32) * 2.0 / values.shape[-1]))
    angle = positions.astype(jnp.float32)[..., None] * freq
    angle = jnp.concatenate([angle, angle], -1)[:, :, None, :]
    turned = jnp.concatenate([-values[..., half:], values[..., :half]], -1)
    return values * jnp.cos(angle) + turned * jnp.sin(angle)


def on_device(
    hidden,
    norm_gain,
    w_query,
    w_key,
    w_value,
    bias_query,
    bias_key,
    bias_value,
    key_pages,
    value_pages,
    kv_lengths,
    page_table,
):
    shards = (
        w_query.astype(jnp.bfloat16),
        w_key.astype(jnp.bfloat16),
        w_value.astype(jnp.bfloat16),
    )
    whole = lax.all_gather(hidden, "tp", axis=2, tiled=True)
    count, steps, width = whole.shape
    wide = whole.astype(jnp.float32)
    power = jnp.mean(wide * wide, axis=2, keepdims=True)
    normed = (
        (wide * lax.rsqrt(power + EPS) * norm_gain)
        .astype(jnp.bfloat16)
        .reshape(count * steps, width)
    )
    local = (
        lax.all_to_all(shards[0], "tp", split_axis=1, concat_axis=0, tiled=True),
        lax.all_to_all(shards[1], "tp", split_axis=1, concat_axis=0, tiled=True),
        lax.all_to_all(shards[2], "tp", split_axis=1, concat_axis=0, tiled=True),
    )
    pieces = (
        lax.all_gather(local[0], "replica", axis=0, tiled=True),
        lax.all_gather(local[1], "replica", axis=0, tiled=True),
        lax.all_gather(local[2], "replica", axis=0, tiled=True),
    )
    sums = tuple((jnp.dot(normed, piece, preferred_element_type=jnp.float32) for piece in pieces))
    made = [
        (total + bias).astype(jnp.bfloat16).reshape(count, steps, -1)
        for total, bias in zip(sums, (bias_query, bias_key, bias_value))
    ]
    query, key_new, value_new = (
        lax.all_to_all(made[0], "tp", split_axis=0, concat_axis=2, tiled=True),
        lax.all_to_all(made[1], "tp", split_axis=0, concat_axis=2, tiled=True),
        lax.all_to_all(made[2], "tp", split_axis=0, concat_axis=2, tiled=True),
    )
    rows = query.shape[0]
    steps = query.shape[1]
    query = query.reshape(rows, steps, HQ, HD)
    key_new = key_new.reshape(rows, steps, KVH, HD)
    value_new = value_new.reshape(rows, steps, KVH, HD)
    positions = kv_lengths[:, None] + jnp.arange(steps, dtype=jnp.int32)[None, :]
    query_rot = rotate(query.astype(jnp.float32), positions).astype(jnp.bfloat16)
    key_rot = rotate(key_new.astype(jnp.float32), positions).astype(jnp.bfloat16)
    group = HQ // KVH
    scale = 1.0 / HD**0.5
    q_heads = query_rot.reshape(rows, steps, KVH, group, HD)
    keys = jnp.take(key_pages, page_table, axis=0)
    vals = jnp.take(value_pages, page_table, axis=0)
    cache = (
        jnp.einsum("rtkgd,rmknd->rtkgmn", q_heads, keys, preferred_element_type=jnp.float32) * scale
    )
    spot = jnp.arange(MOSTP)[:, None] * PAGE + jnp.arange(PAGE)[None, :]
    live = (spot[None] < kv_lengths[:, None, None])[:, None, None, None]
    cache = jnp.where(live, cache, -1e30)
    causal = jnp.arange(steps)[None, :] <= jnp.arange(steps)[:, None]
    fresh = (
        jnp.einsum("rtkgd,rskd->rtkgs", q_heads, key_rot, preferred_element_type=jnp.float32)
        * scale
    )
    fresh = jnp.where(causal[None, :, None, None, :], fresh, -1e30)
    top = jnp.maximum(jnp.max(cache, axis=(4, 5)), jnp.max(fresh, axis=4))
    e_cache = jnp.where(live, jnp.exp(cache - top[..., None, None]), 0.0)
    e_fresh = jnp.where(causal[None, :, None, None, :], jnp.exp(fresh - top[..., None]), 0.0)
    total = jnp.sum(e_cache, axis=(4, 5)) + jnp.sum(e_fresh, axis=4)
    w_cache = (e_cache / total[..., None, None]).astype(jnp.bfloat16)
    w_fresh = (e_fresh / total[..., None]).astype(jnp.bfloat16)
    out = jnp.einsum("rtkgmn,rmknd->rtkgd", w_cache, vals, preferred_element_type=jnp.float32)
    out = out + jnp.einsum(
        "rtkgs,rskd->rtkgd", w_fresh, value_new, preferred_element_type=jnp.float32
    )
    return out.reshape(rows, steps, HQ * HD).astype(jnp.bfloat16)


def solution(mesh):
    in_specs = (
        P("replica", None, "tp"),
        P(),
        P(("replica", "tp"), None),
        P(("replica", "tp"), None),
        P(("replica", "tp"), None),
        P("tp"),
        P("tp"),
        P("tp"),
        P(("replica", "tp"), None, None, None),
        P(("replica", "tp"), None, None, None),
        P(("replica", "tp")),
        P(("replica", "tp"), None),
    )
    out_specs = P(("replica", "tp"), None, None)
    return jax.shard_map(
        on_device, mesh=mesh, in_specs=in_specs, out_specs=out_specs, check_vma=False
    )
```

profile of v0, /device:TPU:0, one launch (start us, length us, event | category | flops | bytes accessed | tf_op | source)
XLA Modules:
  0.0 380.4 jit_solution(5661806267189946849)
XLA Ops:
  6.5 0.0 copy-start
  6.5 0.0 all-gather.6.cloned.1.call-start
  6.5 1.3 copy.32
  7.9 10.0 %all_to_all.90 = bf16[256,4,128]{0,2,1:T(8,128)(2,1)S(1)} all-to-all(bf16[256,4,128]{0,2,1:T(8,128)(2,1)S(1)} %bitcast.101), channel_id=1, replica_groups=mesh['replica'=8,'tp'=4] {'tp'}, dimensions={1} | all-to-all | bytes 524288 | tf_op jit(solution)/shard_map/all_to_all | solution.py:54
  17.9 0.8 copy.33
  18.8 0.0 all-gather.6.cloned.1.call-update
  18.8 0.0 all-gather.8.cloned.1.call-start
  18.8 0.0 copy-done.2
  18.8 0.1 copy.37
  19.0 8.4 %all_to_all.91 = bf16[256,4,128]{0,2,1:T(8,128)(2,1)S(1)} all-to-all(bf16[256,4,128]{0,2,1:T(8,128)(2,1)S(1)} %bitcast.102), channel_id=1, replica_groups=mesh['replica'=8,'tp'=4] {'tp'}, dimensions={1} | all-to-all | bytes 524288 | tf_op jit(solution)/shard_map/all_to_all | solution.py:55
  27.4 0.9 copy.38
  28.2 0.0 all-gather.8.cloned.1.call-update
  28.3 0.0 all-gather.4.cloned.1.call-start
  28.3 4.6 %copy.27 = bf16[256,4096]{0,1:T(8,128)(2,1)} copy(f32[256,4096]{1,0:T(8,128)} %param.16) | data formatting | bytes 6291456 | tf_op args[2]
  32.9 30.1 %all_to_all.92 = bf16[256,4,1024]{0,2,1:T(8,128)(2,1)} all-to-all(bf16[256,4,1024]{0,2,1:T(8,128)(2,1)} %bitcast.96), channel_id=1, replica_groups=mesh['replica'=8,'tp'=4] {'tp'}, dimensions={1} | all-to-all | bytes 4194304 | tf_op jit(solution)/shard_map/all_to_all | solution.py:53
  63.1 4.0 %copy.28 = bf16[4,256,1024]{2,1,0:T(8,128)(2,1)} copy(bf16[4,256,1024]{1,2,0:T(8,128)(2,1)} %bitcast.98) | data formatting | bytes 4194304 | tf_op jit(solution)/shard_map/all_to_all | solution.py:53
  67.0 0.0 all-gather.4.cloned.1.call-update
  67.1 0.9 copy-done.3
  68.0 7.8 %all_gather.12 = bf16[12,4,8192]{2,1,0:T(4,128)(2,1)S(1)} all-gather(bf16[12,4,2048]{2,1,0:T(4,128)(2,1)S(1)} %copy-done.3), channel_id=1, replica_groups=mesh['replica'=8,'tp'=4] {'tp'}, dimensions={2}, use_global_device_ids=true | all-gather | bytes 983040 | tf_op jit(solution)/shard_map/all_gather | solution.py:43
  75.8 0.5 fusion.6
  76.3 0.0 copy-done.4
  76.3 1.4 fusion.8
  77.7 1.6 reshape.170
  79.3 0.0 copy-done.5
  79.3 0.1 reshape.199
  79.4 0.0 copy-done
  79.4 2.7 gather_fusion.1
  82.2 4.3 %gather_fusion = bf16[24,4,128,128]{3,2,1,0:T(8,128)(2,1)} fusion(bf16[16,4,128,128]{3,2,1,0:T(8,128)(2,1)} %param.23, s32[1024]{0:T(1024)S(1)} %pad_clamp_fusion), kind=kCustom, calls=%fused_computation.clone | custom fusion | bytes 6291552 | tf_op jit(solution)/shard_map/jit(_take)/gather | solution.py:84
  86.5 0.0 copy-done.7
  86.5 0.1 add_convert_fusion
  86.6 0.1 broadcast_multiply_fusion
  86.7 0.1 fusion.47
  86.8 0.1 iota_add_fusion
  86.9 0.1 broadcast_compare_fusion
  87.0 0.0 copy-done.8
  87.0 2.7 fusion.24
  89.6 3.4 all-to-all-start.3
  93.0 25.1 %all-gather.8.cloned.1.call-done = bf16[8192,128]{1,0:T(8,128)(2,1)} async-done(((bf16[1024,128]{1,0:T(8,128)(2,1)}), bf16[8192,128]{1,0:T(8,128)(2,1)}) %all-gather.8.cloned.1.call-update) | async-done | bytes 2097168 | tf_op jit(solution)/shard_map/all_gather | solution.py:60
  118.2 0.0 copy-done.9
  118.2 2.7 fusion.25
  120.8 0.0 all-to-all-done.3
  120.8 225.3 %all-gather.4.cloned.1.call-done = bf16[8192,1024]{1,0:T(8,128)(2,1)} async-done(((bf16[1024,1024]{1,0:T(8,128)(2,1)}), bf16[8192,1024]{1,0:T(8,128)(2,1)}) %all-gather.4.cloned.1.call-update) | async-done | bytes 16777232 | tf_op jit(solution)/shard_map/all_gather | solution.py:58
  346.1 0.0 copy-done.6
  346.1 8.8 %fusion.19 = bf16[48,1024]{1,0:T(8,128)(2,1)S(1)} fusion(bf16[48,8192]{1,0:T(8,128)(2,1)S(1)} %reshape.170, bf16[8192,1024]{1,0:T(8,128)(2,1)} %all-gather.4.cloned.1.call-done, f32[1024]{0:T(1024)S(1)} %copy-done.6), kind=kOutput, calls=%fused_computation.27 | convolution fusion | flops 805404672 | bytes 17666048 | tf_op jit(solution)/shard_map/dot_general | solution.py:62
  354.9 0.7 reshape.171
  355.6 3.3 all-to-all-start.1
  358.9 0.1 slice_negate_fusion.1
  359.0 4.2 %all-to-all-done.1 = bf16[12,4,1024]{2,1,0:T(4,128)(2,1)S(1)} async-done(((bf16[12,4,1024]{2,1,0:T(4,128)(2,1)}), bf16[12,4,1024]{2,1,0:T(4,128)(2,1)S(1)}, u32[]{:S(2)}, u32[]{:S(2)}) %all-to-all-start.1) | async-done | bytes 98336 | tf_op jit(solution)/shard_map/all_to_all | solution.py:68
  363.2 3.4 all-to-all-start.5
  366.6 0.1 copy.30
  366.8 0.1 reshape.174
  366.9 0.1 reshape.175
  367.0 0.1 fusion.30
  367.1 0.1 fusion.32
  367.2 0.6 fusion.52
  367.8 0.0 copy-start.1
  367.8 3.4 bitcast_reduce_fusion
  371.2 0.2 fusion.35
  371.4 0.4 fusion.15
  371.8 0.0 copy-done.1
  371.8 1.0 fusion.16
  372.8 0.0 all-to-all-done.5
  372.8 0.3 fusion.21
  373.2 0.7 convert_element_type.107
  (21 shorter events, 0.1 us)
Async XLA Ops:
  6.5 72.9 %copy-start = (bf16[16,4,128,128]{3,2,1,0:T(8,128)(2,1)S(1)}, bf16[16,4,128,128]{3,2,1,0:T(8,128)(2,1)}, u32[]{:S(2)}) copy-start(bf16[16,4,128,128]{3,2,1,0:T(8,128)(2,1)} %param.22) | copy-start | bytes 6291460
  6.5 12.3 %copy-start.2 = (f32[256,512]{1,0:T(8,128)S(1)}, f32[256,512]{1,0:T(8,128)}, u32[]{:S(2)}) copy-start(f32[256,512]{1,0:T(8,128)} %param.18) | copy-start | bytes 1572868
  6.5 80.4 %all-gather.6.cloned.1.call-start = ((), (), s32[]{:S(2)}) async-start(), calls=%async_computation.7 | async-start | bytes 2359296 | tf_op jit(solution)/shard_map/all_gather | solution.py:59
  18.8 99.4 %all-gather.8.cloned.1.call-start = ((), (), s32[]{:S(2)}) async-start(), calls=%async_computation.8 | async-start | bytes 2359296 | tf_op jit(solution)/shard_map/all_gather | solution.py:60
  28.3 317.9 %all-gather.4.cloned.1.call-start = ((), (), s32[]{:S(2)}) async-start(), calls=%async_computation.6 | async-start | bytes 18874368 | tf_op jit(solution)/shard_map/all_gather | solution.py:58
  67.0 0.9 copy-start.3
  67.0 9.3 %copy-start.4 = (f32[8192]{0:T(1024)S(1)}, f32[8192]{0:T(1024)}, u32[]{:S(2)}) copy-start(f32[8192]{0:T(1024)} %param.15) | copy-start | bytes 98308
  75.8 3.5 copy-start.5
  82.2 4.4 %copy-start.7 = (s32[3]{0:T(128)S(1)}, s32[3]{0:T(128)}, u32[]{:S(2)}) copy-start(s32[3]{0:T(128)} %param.24) | copy-start | bytes 40
  82.2 4.8 %copy-start.8 = (f32[128]{0:T(128)S(1)}, f32[128]{0:T(128)}, u32[]{:S(2)}) copy-start(f32[128]{0:T(128)} %param.20) | copy-start | bytes 1540
  86.5 31.7 %copy-start.9 = (f32[128]{0:T(128)S(1)}, f32[128]{0:T(128)}, u32[]{:S(2)}) copy-start(f32[128]{0:T(128)} %param.21) | copy-start | bytes 1540
  89.6 256.5 %copy-start.6 = (f32[1024]{0:T(1024)S(1)}, f32[1024]{0:T(1024)}, u32[]{:S(2)}) copy-start(f32[1024]{0:T(1024)} %param.19) | copy-start | bytes 12292
  89.6 31.2 %all-to-all-start.3 = ((bf16[12,4,128]{2,1,0:T(4,128)(2,1)}), bf16[12,4,128]{2,1,0:T(4,128)(2,1)S(1)}, u32[]{:S(2)}, u32[]{:S(2)}) async-start(bf16[12,4,128]{2,1,0:T(4,128)(2,1)} %bitcast.19), calls=%async_computation.3 | async-start | bytes 24576 | tf_op jit(solution)/shard_map/all_to_all | solution.py:69
  355.6 7.6 %all-to-all-start.1 = ((bf16[12,4,1024]{2,1,0:T(4,128)(2,1)}), bf16[12,4,1024]{2,1,0:T(4,128)(2,1)S(1)}, u32[]{:S(2)}, u32[]{:S(2)}) async-start(bf16[12,4,1024]{2,1,0:T(4,128)(2,1)} %reshape.171), calls=%async_computation.1 | async-start | bytes 196608 | tf_op jit(solution)/shard_map/all_to_all | solution.py:68
  363.2 9.6 %all-to-all-start.5 = ((bf16[12,4,128]{2,1,0:T(4,128)(2,1)}), bf16[12,4,128]{2,1,0:T(4,128)(2,1)S(1)}, u32[]{:S(2)}, u32[]{:S(2)}) async-start(bf16[12,4,128]{2,1,0:T(4,128)(2,1)} %bitcast.30), calls=%async_computation.5 | async-start | bytes 24576 | tf_op jit(solution)/shard_map/all_to_all | solution.py:70
  367.8 4.0 %copy-start.1 = (bf16[24,4,128,128]{3,2,1,0:T(8,128)(2,1)S(1)}, bf16[24,4,128,128]{3,2,1,0:T(8,128)(2,1)}, u32[]{:S(2)}) copy-start(bf16[24,4,128,128]{3,2,1,0:T(8,128)(2,1)} %gather_fusion) | copy-start | bytes 9437188
Sparse Core Ops, SparseCore 0:
  18.9 49.3 all-gather.5
  70.5 47.6 all-gather.7
  120.3 225.7 all-gather.3
where the time goes:
time: 381 us; the launch traced here: 380 us
  waiting for transfers between devices  255 us (67%)
  blocking collectives  56.4 us (15%)
  local copies, waits for them, and re-layouts  23.1 us (6%)
  matrix products  19.4 us (5%)
  between operations  13.4 us (4%)
  starting transfers between devices  10.2 us (3%)
    all_gather x1, waiting for transfers between devices, on_device(): lax.all_gather(local[0], 'replica', axis=0, tiled=True)  225 us
    all_to_all x1, blocking collectives, on_device(): lax.all_to_all(shards[0], 'tp', split_axis=1, concat_axis=0, tiled=True)  30.1 us
    all_gather x1, waiting for transfers between devices, on_device(): lax.all_gather(local[2], 'replica', axis=0, tiled=True)  25.1 us
    dot_general x3, matrix products, on_device(): jnp.dot(normed, piece, preferred_element_type=jnp.float32)  14.1 us
    all_to_all x1, blocking collectives, on_device(): lax.all_to_all(shards[1], 'tp', split_axis=1, concat_axis=0, tiled=True)  10 us
    all_to_all x1, blocking collectives, on_device(): lax.all_to_all(shards[2], 'tp', split_axis=1, concat_axis=0, tiled=True)  8.39 us
    all_gather x1, blocking collectives, on_device(): whole = lax.all_gather(hidden, 'tp', axis=2, tiled=True)  7.81 us
  transfers between devices with their start and end apart: 6, of which 3 were waited for; matrix products, arithmetic and copies ran while one was open for 8% of the time, Pallas kernels for 0%

commit v1 on v0

--- a/solution.py
+++ b/solution.py
@@ -1,3 +1,4 @@
+import functools
 import jax
 import jax.numpy as jnp
 from jax import lax
@@ -10,6 +11,35 @@
 MOSTP = 8
 EPS = 1e-06
 THETA = 1000000.0
+
+
+def reach_frames(piece_in, d0):
+    amount_of = lax.axis_size("replica")
+    in_order = []
+    j = 0
+    while j < amount_of:
+        in_order.append((j, (j + 1) % amount_of))
+        j += 1
+    panels = []
+    j = 0
+    while j < amount_of:
+        panels.append((j, (j - 1) % amount_of))
+        j = j + 1
+    x_now, block_next = ([piece_in], [piece_in])
+    for _ in range(amount_of // 2):
+        x_now.append(lax.ppermute(x_now[-1], "replica", in_order))
+    no = 0
+    while no < (amount_of - 1) // 2:
+        block_next.append(lax.ppermute(block_next[-1], "replica", panels))
+        no += 1
+    return jnp.roll(
+        jnp.concatenate([*x_now[::-1], *block_next[1:]], axis=d0),
+        (lax.axis_index("replica") - amount_of // 2) * piece_in.shape[d0],
+        axis=d0,
+    )
+
+
+keep_up_point_here = functools.partial(reach_frames, d0=0)
 
 
 def rotate(values, positions):
@@ -55,7 +85,7 @@
         lax.all_to_all(shards[2], "tp", split_axis=1, concat_axis=0, tiled=True),
     )
     pieces = (
-        lax.all_gather(local[0], "replica", axis=0, tiled=True),
+        keep_up_point_here(local[0]),
         lax.all_gather(local[1], "replica", axis=0, tiled=True),
         lax.all_gather(local[2], "replica", axis=0, tiled=True),
     )

time: 381 us -> 484 us (1.27)
  local copies, waits for them, and re-layouts: 23.1 us -> 68.5 us
  waiting for transfers between devices: 255 us -> 289 us
  starting transfers between devices: 10.2 us -> 41.4 us
  blocking collectives: 56.4 us -> 47.7 us
    ppermute x0 -> x7, waiting for transfers between devices: none -> 249 us  [the longest x4 247 us: reach_frames(): x_now.append(lax.ppermute(x_now[-1], 'replica', in_order))]
    all_gather x1 -> x0, waiting for transfers between devices: 225 us -> none  [on_device(): lax.all_gather(local[0], 'replica', axis=0, tiled=True)]
    unnamed x23 -> x42, local copies, waits for them, and re-layouts: 7.03 us -> 49.3 us
    ppermute x0 -> x7, starting transfers between devices: none -> 28 us  [the longest x3 20.7 us: reach_frames(): block_next.append(lax.ppermute(block_next[-1], 'replica', panels))]
    all_gather x1, waiting for transfers between devices: 25.1 us -> 35.5 us  [on_device(): lax.all_gather(local[2], 'replica', axis=0, tiled=True)]
    all_to_all x1 -> x0, blocking collectives: 8.39 us -> none  [on_device(): lax.all_to_all(shards[2], 'tp', split_axis=1, concat_axis=0, tiled=True)]
  transfers between devices with their start and end apart: 6 -> 13, of which waited for: 3 -> 7; matrix products, arithmetic and copies ran while one was open for 8% -> 9% of each run, Pallas kernels for 0% -> 0%
where the time goes in v1:
time: 484 us; the launch traced here: 483 us
  waiting for transfers between devices  289 us (60%)
  local copies, waits for them, and re-layouts  68.5 us (14%)
  blocking collectives  47.7 us (10%)
  starting transfers between devices  41.4 us (9%)
  matrix products  19.3 us (4%)
  between operations  13.7 us (3%)
    ppermute x4, waiting for transfers between devices, reach_frames(): x_now.append(lax.ppermute(x_now[-1], 'replica', in_order))  247 us
    unnamed x42, local copies, waits for them, and re-layouts  49.3 us
    all_gather x1, waiting for transfers between devices, on_device(): lax.all_gather(local[2], 'replica', axis=0, tiled=True)  35.5 us
    all_to_all x1, blocking collectives, on_device(): lax.all_to_all(shards[0], 'tp', split_axis=1, concat_axis=0, tiled=True)  30.8 us
    ppermute x3, starting transfers between devices, reach_frames(): block_next.append(lax.ppermute(block_next[-1], 'replica', panels))  20.7 us
    dot_general x3, matrix products, on_device(): jnp.dot(normed, piece, preferred_element_type=jnp.float32)  14.1 us
  transfers between devices with their start and end apart: 13, of which 7 were waited for; matrix products, arithmetic and copies ran while one was open for 9% of the time, Pallas kernels for 0%

profile of v1, /device:TPU:0, one launch (start us, length us, event | category | flops | bytes accessed | tf_op | source)
XLA Modules:
  0.0 482.8 jit_solution(1587899412225080560)
XLA Ops:
  6.5 4.8 copy.27
  11.3 30.8 %all_to_all.90 = bf16[256,4,1024]{0,2,1:T(8,128)(2,1)} all-to-all(bf16[256,4,1024]{0,2,1:T(8,128)(2,1)} %bitcast.99), channel_id=1, replica_groups=mesh['replica'=8,'tp'=4] {'tp'}, dimensions={1} | all-to-all | bytes 4194304 | tf_op jit(solution)/shard_map/all_to_all | solution.py:83
  42.1 4.1 copy.28
  46.2 2.3 collective-permute-start
  48.5 0.1 copy.32
  48.7 8.4 %all_to_all.91 = bf16[256,4,128]{0,2,1:T(8,128)(2,1)S(1)} all-to-all(bf16[256,4,128]{0,2,1:T(8,128)(2,1)S(1)} %bitcast.103), channel_id=1, replica_groups=mesh['replica'=8,'tp'=4] {'tp'}, dimensions={1} | all-to-all | bytes 524288 | tf_op jit(solution)/shard_map/all_to_all | solution.py:84
  57.0 0.8 copy.33
  57.9 47.7 %collective-permute-done = bf16[1024,1024]{1,0:T(8,128)(2,1)} collective-permute-done((bf16[1024,1024]{1,0:T(8,128)(2,1)}, bf16[1024,1024]{1,0:T(8,128)(2,1)}, u32[]{:S(2)}, u32[]{:S(2)}) %collective-permute-start) | collective-permute-done | bytes 2097184 | tf_op jit(solution)/shard_map/ppermute | solution.py:30
  105.6 4.7 collective-permute-start.4
  110.3 0.8 copy.37
  111.1 3.4 all-to-all-start.4
  114.6 91.7 %collective-permute-done.1 = bf16[1024,1024]{1,0:T(8,128)(2,1)} collective-permute-done((bf16[1024,1024]{1,0:T(8,128)(2,1)}, bf16[1024,1024]{1,0:T(8,128)(2,1)}, u32[]{:S(2)}, u32[]{:S(2)}) %collective-permute-start.1) | collective-permute-done | bytes 2097184 | tf_op jit(solution)/shard_map/ppermute | solution.py:30
  206.3 2.5 collective-permute-start.2
  208.8 8.5 %all_gather.9 = bf16[12,4,8192]{2,1,0:T(4,128)(2,1)S(1)} all-gather(bf16[12,4,2048]{2,1,0:T(4,128)(2,1)} %param.14), channel_id=1, replica_groups=mesh['replica'=8,'tp'=4] {'tp'}, dimensions={2}, use_global_device_ids=true | all-gather | bytes 983040 | tf_op jit(solution)/shard_map/all_gather | solution.py:73
  217.3 0.1 reshape.199
  217.4 0.5 fusion.8
  217.9 0.8 copy.38
  219.1 14.4 %collective-permute-start.5 = (bf16[1024,1024]{1,0:T(8,128)(2,1)}, bf16[1024,1024]{1,0:T(8,128)(2,1)}, u32[]{:S(2)}, u32[]{:S(2)}) collective-permute-start(bf16[1024,1024]{1,0:T(8,128)(2,1)} %collective-permute-done.4), channel_id=1, source_target_pairs={{0,28},{4,0},{8,4},{12,8},{16,12},{20,16},{24,20},{28,24},{1,29},{... | collective-permute-start | bytes 6291464 | tf_op jit(solution)/shard_map/ppermute | solution.py:33
  233.5 79.6 %collective-permute-done.2 = bf16[1024,1024]{1,0:T(8,128)(2,1)} collective-permute-done((bf16[1024,1024]{1,0:T(8,128)(2,1)}, bf16[1024,1024]{1,0:T(8,128)(2,1)}, u32[]{:S(2)}, u32[]{:S(2)}) %collective-permute-start.2) | collective-permute-done | bytes 2097184 | tf_op jit(solution)/shard_map/ppermute | solution.py:30
  313.1 2.5 collective-permute-start.3
  315.6 1.4 fusion.10
  317.0 2.1 collective-permute-done.5
  319.0 1.6 collective-permute-start.6
  320.6 1.6 reshape.170
  322.2 2.7 gather_fusion.1
  324.9 4.3 gather_fusion
  329.2 0.1 fusion.54
  329.4 2.7 fusion.31
  332.1 3.4 all-to-all-start.3
  335.5 35.5 %all-gather.5.cloned.1.call-done = bf16[8192,128]{1,0:T(8,128)(2,1)} async-done(((bf16[1024,128]{1,0:T(8,128)(2,1)}), bf16[8192,128]{1,0:T(8,128)(2,1)}) %all-gather.5.cloned.1.call-update) | async-done | bytes 2097168 | tf_op jit(solution)/shard_map/all_gather | solution.py:90
  371.0 2.7 fusion.32
  373.7 28.2 %collective-permute-done.3 = bf16[1024,1024]{1,0:T(8,128)(2,1)} collective-permute-done((bf16[1024,1024]{1,0:T(8,128)(2,1)}, bf16[1024,1024]{1,0:T(8,128)(2,1)}, u32[]{:S(2)}, u32[]{:S(2)}) %collective-permute-start.3) | collective-permute-done | bytes 2097184 | tf_op jit(solution)/shard_map/ppermute | solution.py:30
  401.9 3.1 constant_dynamic-update-slice_fusion.15
  405.0 3.1 constant_dynamic-update-slice_fusion.14
  408.0 3.2 constant_dynamic-update-slice_fusion.13
  411.3 3.1 constant_dynamic-update-slice_fusion.12
  414.4 1.6 constant_dynamic-update-slice_fusion.11
  416.0 3.1 constant_dynamic-update-slice_fusion.10
  419.1 3.1 constant_dynamic-update-slice_fusion.9
  422.2 3.1 constant_dynamic-update-slice_fusion.8
  425.2 3.1 constant_dynamic-update-slice_fusion.7
  428.3 3.1 constant_dynamic-update-slice_fusion.6
  431.4 3.1 constant_dynamic-update-slice_fusion.5
  434.5 3.1 constant_dynamic-update-slice_fusion.4
  437.6 1.6 constant_dynamic-update-slice_fusion.3
  439.2 3.1 constant_dynamic-update-slice_fusion.2
  442.3 3.1 constant_dynamic-update-slice_fusion.1
  445.4 3.1 constant_dynamic-update-slice_fusion
  448.5 8.8 %fusion.24 = bf16[48,1024]{1,0:T(8,128)(2,1)S(1)} fusion(bf16[48,8192]{1,0:T(8,128)(2,1)S(1)} %reshape.170, bf16[16384,1024]{1,0:T(8,128)(2,1)} %constant_dynamic-update-slice_fusion, s32[]{:T(128)S(6)} %select_n.38, f32[1024]{0:T(1024)S(1)} %copy-done.11), kind=kOutput, calls=%fused_computation.29 | convolution fusion | flops 805404672 | bytes 17666052 | tf_op jit(solution)/shard_map/dot_general | solution.py:92
  457.3 0.7 reshape.171
  457.9 3.3 all-to-all-start.1
  461.3 4.2 all-to-all-done.1
  465.5 3.2 all-to-all-start.5
  468.8 0.1 copy.30
  468.9 0.1 reshape.174
  469.1 0.1 fusion.37
  469.2 0.1 fusion.39
  469.4 0.6 fusion.60
  470.0 3.4 bitcast_reduce_fusion
  473.3 0.2 fusion.42
  473.5 0.4 fusion.17
  474.0 1.0 fusion.18
  475.0 0.3 fusion.28
  475.3 0.7 convert_element_type.107
  (53 shorter events, 0.7 us)
Async XLA Ops:
  6.5 315.7 %copy-start = (bf16[16,4,128,128]{3,2,1,0:T(8,128)(2,1)S(1)}, bf16[16,4,128,128]{3,2,1,0:T(8,128)(2,1)}, u32[]{:S(2)}) copy-start(bf16[16,4,128,128]{3,2,1,0:T(8,128)(2,1)} %param.22) | copy-start | bytes 6291460
  6.5 322.9 %all-gather.3.cloned.1.call-start = ((), (), s32[]{:S(2)}) async-start(), calls=%async_computation.6 | async-start | bytes 2359296 | tf_op jit(solution)/shard_map/all_gather | solution.py:89
  42.1 6.4 %copy-start.4 = (f32[256,512]{1,0:T(8,128)S(1)}, f32[256,512]{1,0:T(8,128)}, u32[]{:S(2)}) copy-start(f32[256,512]{1,0:T(8,128)} %param.17) | copy-start | bytes 1572868
  42.1 68.2 %copy-start.5 = (f32[256,512]{1,0:T(8,128)S(1)}, f32[256,512]{1,0:T(8,128)}, u32[]{:S(2)}) copy-start(f32[256,512]{1,0:T(8,128)} %param.18) | copy-start | bytes 1572868
  42.1 72.5 %copy-start.7 = (s32[3,8]{1,0:T(4,128)S(1)}, s32[3,8]{1,0:T(4,128)}, u32[]{:S(2)}) copy-start(s32[3,8]{1,0:T(4,128)} %param.25) | copy-start | bytes 292
  46.2 172.6 %copy-start.8 = (s32[3]{0:T(128)S(1)}, s32[3]{0:T(128)}, u32[]{:S(2)}) copy-start(s32[3]{0:T(128)} %param.24) | copy-start | bytes 40
  46.2 269.4 %copy-start.6 = (f32[8192]{0:T(1024)S(1)}, f32[8192]{0:T(1024)}, u32[]{:S(2)}) copy-start(f32[8192]{0:T(1024)} %param.15) | copy-start | bytes 98308
  46.2 59.4 %collective-permute-start = (bf16[1024,1024]{1,0:T(8,128)(2,1)}, bf16[1024,1024]{1,0:T(8,128)(2,1)}, u32[]{:S(2)}, u32[]{:S(2)}) collective-permute-start(bf16[1024,1024]{1,0:T(8,128)(2,1)} %bitcast.95), channel_id=1, source_target_pairs={{0,4},{4,8},{8,12},{12,16},{16,20},{20,24},{24,28},{28,0},{1,5},{5... | collective-permute-start | bytes 6291464 | tf_op jit(solution)/shard_map/ppermute | solution.py:30
  105.6 100.7 %collective-permute-start.1 = (bf16[1024,1024]{1,0:T(8,128)(2,1)}, bf16[1024,1024]{1,0:T(8,128)(2,1)}, u32[]{:S(2)}, u32[]{:S(2)}) collective-permute-start(bf16[1024,1024]{1,0:T(8,128)(2,1)} %collective-permute-done), channel_id=1, source_target_pairs={{0,4},{4,8},{8,12},{12,16},{16,20},{20,24},{24,28},{28,0},{1,5},{5... | collective-permute-start | bytes 6291464 | tf_op jit(solution)/shard_map/ppermute | solution.py:30
  105.6 113.5 %collective-permute-start.4 = (bf16[1024,1024]{1,0:T(8,128)(2,1)}, bf16[1024,1024]{1,0:T(8,128)(2,1)}, u32[]{:S(2)}, u32[]{:S(2)}) collective-permute-start(bf16[1024,1024]{1,0:T(8,128)(2,1)} %bitcast.96), channel_id=1, source_target_pairs={{0,28},{4,0},{8,4},{12,8},{16,12},{20,16},{24,20},{28,24},{1,29},{... | collective-permute-start | bytes 6291464 | tf_op jit(solution)/shard_map/ppermute | solution.py:33
  111.1 106.8 %all-to-all-start.4 = ((bf16[256,4,128]{0,2,1:T(8,128)(2,1)}), bf16[256,4,128]{0,2,1:T(8,128)(2,1)S(1)}, u32[]{:S(2)}, u32[]{:S(2)}) async-start(bf16[256,4,128]{0,2,1:T(8,128)(2,1)} %bitcast.27), calls=%async_computation.4 | async-start | bytes 524288 | tf_op jit(solution)/shard_map/all_to_all | solution.py:85
  114.6 256.5 %all-gather.5.cloned.1.call-start = ((), (), s32[]{:S(2)}) async-start(), calls=%async_computation.7 | async-start | bytes 2359296 | tf_op jit(solution)/shard_map/all_gather | solution.py:90
  206.3 106.8 %collective-permute-start.2 = (bf16[1024,1024]{1,0:T(8,128)(2,1)}, bf16[1024,1024]{1,0:T(8,128)(2,1)}, u32[]{:S(2)}, u32[]{:S(2)}) collective-permute-start(bf16[1024,1024]{1,0:T(8,128)(2,1)} %collective-permute-done.1), channel_id=1, source_target_pairs={{0,4},{4,8},{8,12},{12,16},{16,20},{20,24},{24,28},{28,0},{1,5},{5... | collective-permute-start | bytes 6291464 | tf_op jit(solution)/shard_map/ppermute | solution.py:30
  219.1 99.9 %collective-permute-start.5 = (bf16[1024,1024]{1,0:T(8,128)(2,1)}, bf16[1024,1024]{1,0:T(8,128)(2,1)}, u32[]{:S(2)}, u32[]{:S(2)}) collective-permute-start(bf16[1024,1024]{1,0:T(8,128)(2,1)} %collective-permute-done.4), channel_id=1, source_target_pairs={{0,28},{4,0},{8,4},{12,8},{16,12},{20,16},{24,20},{28,24},{1,29},{... | collective-permute-start | bytes 6291464 | tf_op jit(solution)/shard_map/ppermute | solution.py:33
  313.1 88.8 %collective-permute-start.3 = (bf16[1024,1024]{1,0:T(8,128)(2,1)}, bf16[1024,1024]{1,0:T(8,128)(2,1)}, u32[]{:S(2)}, u32[]{:S(2)}) collective-permute-start(bf16[1024,1024]{1,0:T(8,128)(2,1)} %collective-permute-done.2), channel_id=1, source_target_pairs={{0,4},{4,8},{8,12},{12,16},{16,20},{20,24},{24,28},{28,0},{1,5},{5... | collective-permute-start | bytes 6291464 | tf_op jit(solution)/shard_map/ppermute | solution.py:30
  319.0 103.1 %collective-permute-start.6 = (bf16[1024,1024]{1,0:T(8,128)(2,1)}, bf16[1024,1024]{1,0:T(8,128)(2,1)}, u32[]{:S(2)}, u32[]{:S(2)}) collective-permute-start(bf16[1024,1024]{1,0:T(8,128)(2,1)} %collective-permute-done.5), channel_id=1, source_target_pairs={{0,28},{4,0},{8,4},{12,8},{16,12},{20,16},{24,20},{28,24},{1,29},{... | collective-permute-start | bytes 6291464 | tf_op jit(solution)/shard_map/ppermute | solution.py:33
  324.9 4.5 copy-start.9
  324.9 46.1 %copy-start.10 = (f32[128]{0:T(128)S(1)}, f32[128]{0:T(128)}, u32[]{:S(2)}) copy-start(f32[128]{0:T(128)} %param.21) | copy-start | bytes 1540
  332.1 41.6 %all-to-all-start.3 = ((bf16[12,4,128]{2,1,0:T(4,128)(2,1)}), bf16[12,4,128]{2,1,0:T(4,128)(2,1)S(1)}, u32[]{:S(2)}, u32[]{:S(2)}) async-start(bf16[12,4,128]{2,1,0:T(4,128)(2,1)} %bitcast.19), calls=%async_computation.3 | async-start | bytes 24576 | tf_op jit(solution)/shard_map/all_to_all | solution.py:99
  408.0 6.4 %copy-start.2 = (bf16[4,256,1024]{2,1,0:T(8,128)(2,1)S(1)}, bf16[4,256,1024]{2,1,0:T(8,128)(2,1)}, u32[]{:S(2)}) copy-start(bf16[4,256,1024]{2,1,0:T(8,128)(2,1)} %copy.28) | copy-start | bytes 6291460
  445.4 3.1 copy-start.11
  457.9 7.6 %all-to-all-start.1 = ((bf16[12,4,1024]{2,1,0:T(4,128)(2,1)}), bf16[12,4,1024]{2,1,0:T(4,128)(2,1)S(1)}, u32[]{:S(2)}, u32[]{:S(2)}) async-start(bf16[12,4,1024]{2,1,0:T(4,128)(2,1)} %reshape.171), calls=%async_computation.1 | async-start | bytes 196608 | tf_op jit(solution)/shard_map/all_to_all | solution.py:98
  465.5 9.5 %all-to-all-start.5 = ((bf16[12,4,128]{2,1,0:T(4,128)(2,1)}), bf16[12,4,128]{2,1,0:T(4,128)(2,1)S(1)}, u32[]{:S(2)}, u32[]{:S(2)}) async-start(bf16[12,4,128]{2,1,0:T(4,128)(2,1)} %bitcast.30), calls=%async_computation.5 | async-start | bytes 24576 | tf_op jit(solution)/shard_map/all_to_all | solution.py:100
  470.0 4.0 copy-start.3
  474.0 2.0 copy-start.1
Sparse Core Ops, SparseCore 0:
  58.0 125.7 all-gather.2
  218.9 152.0 all-gather.4
